TPU v7x, 256 devices: a whole 4x4x8 slice. The times are simulated.
256 devices in a mesh: mem: 16 (over z, core), row: 16 (over x, y).
Axes of the slice: x: 4, y: 4, z: 8, core: 2. Of those that a mesh axis runs over, the one named last changes fastest.
Arguments:
- members: bfloat16 [16, 5, 256, 4096], P('mem', None, 'row'), may hold values from -6 to 6
- enc_first: bfloat16 [64, 5, 3, 3], replicated, may hold values from -0.875 to 0.875
- enc_second: bfloat16 [64, 64, 3, 3], replicated, may hold values from -0.25 to 0.25
- enc_third: bfloat16 [16, 64, 3, 3], replicated, may hold values from -0.25 to 0.25
- mix_weight: bfloat16 [32, 256], replicated, may hold values from -0.375 to 0.375
- dec_first: bfloat16 [32, 32, 4, 4], replicated, may hold values from -0.5 to 0.5
- dec_second: bfloat16 [16, 32, 4, 4], replicated, may hold values from -0.5 to 0.5
Outputs:
- output_field: bfloat16 [16, 256, 4096], P(None, 'row', 'mem')
All inputs are finite; a program needn't handle non-finite values.
Results may differ from a plain program's by a relative error of at most 0.029.
Values may be sent and summed in bfloat16 or wider, within the bound.
A program may use at most 128 MiB of HBM per device.

v0:
```python
import jax
import jax.numpy as jnp
from jax import lax
from jax.experimental import pallas as pl
from jax.experimental.pallas import tpu as pltpu
from jax.sharding import PartitionSpec as P

MESH = pl.DeviceIdType.MESH
BLOCK = 64
EDGE = 32
F32 = jnp.float32
BF16 = jnp.bfloat16


def dot(a, b):
    return jnp.dot(a, b, preferred_element_type=F32)


def silu(v):
    half = 0.5 * v
    return half + half * jnp.tanh(half)


def one_hot(shape, rule):
    rows = lax.broadcasted_iota(jnp.int32, shape, 0)
    cols = lax.broadcasted_iota(jnp.int32, shape, 1)
    return jnp.where(rule(rows, cols), 1.0, 0.0).astype(BF16)


def kernel(
    nm, nr, x_ref, w1_ref, w2_ref, w3_ref, mix_ref, d1_ref, d2_ref, out_ref,
    top, bot, x1s, h1s, h2s, snd, rcv, latx, lats, lath, upx, zz,
    halo_send, halo_recv, a2a_send, a2a_recv, lat_send, lat_recv,
):
    me = lax.axis_index("mem")
    row = lax.axis_index("row")
    above, below = lax.rem(row + nr - 1, nr), lax.rem(row + 1, nr)
    cols = nm * BLOCK

    barrier = pltpu.get_barrier_semaphore()
    for near in (above, below):
        pl.semaphore_signal(barrier, inc=1, device_id={"row": near}, device_id_type=MESH)

    @pl.loop(1, nm)
    def _(step):
        pl.semaphore_signal(
            barrier, inc=1, device_id={"mem": lax.rem(me + step, nm)}, device_id_type=MESH
        )

    pl.semaphore_wait(barrier, nm + 1)

    down = pltpu.make_async_remote_copy(
        x_ref.at[:, pl.ds(8, 8), :], top, halo_send.at[0], halo_recv.at[0],
        device_id={"row": below}, device_id_type=MESH,
    )
    up = pltpu.make_async_remote_copy(
        x_ref.at[:, pl.ds(0, 8), :], bot, halo_send.at[1], halo_recv.at[1],
        device_id={"row": above}, device_id_type=MESH,
    )
    down.start()
    up.start()

    has_above = jnp.where(row > 0, 1.0, 0.0)
    has_below = jnp.where(row < nr - 1, 1.0, 0.0)

    phases = one_hot((512, 512), lambda a, b: a == 4 * (b % 128) + b // 128)
    lane128 = lax.broadcasted_iota(jnp.int32, (1, 128), 1)

    def split(source, select, first, count, scale):
        flat = source.reshape(source.shape[0] * source.shape[1], source.shape[2])
        before = jnp.zeros((select.shape[0], 128), F32)
        zero = jnp.zeros((8, 128), F32)
        for k in range(cols // 128):
            ordered = dot(select, flat[:, 512 * k : 512 * (k + 1)])
            if scale is not None:
                ordered = ordered * scale
            z = dot(ordered.astype(BF16), phases)
            turned = pltpu.roll(z[:, 384:512], 1, 1)
            late = jnp.where(lane128 == 0, before, turned)
            before = turned
            for r in range(count):
                part = slice(8 * r, 8 * r + 8)
                tile = jnp.concatenate(
                    [z[part, 0:128], z[part, 128:256], z[part, 256:384], z[part, 384:512],
                     late[part], zero],
                    axis=0,
                )
                x1s[48 * (first + r) : 48 * (first + r + 1), 128 * k : 128 * (k + 1)] = (
                    tile.astype(BF16)
                )

    split(x_ref[...], one_hot((128, 80), lambda a, b: (a % 8 < 5) & (b == (a % 8) * 16 + a // 8)),
          5, 16, None)
    down.wait()
    up.wait()
    split(top[...], one_hot((48, 40), lambda a, b: (a % 8 < 5) & (a < 40) & (b == (a % 8) * 8 + 3 + a // 8)),
          0, 5, has_above)
    split(bot[...], one_hot((16, 40), lambda a, b: (a % 8 < 5) & (b == (a % 8) * 8 + a // 8)),
          21, 2, has_below)

    lane = lax.broadcasted_iota(jnp.int32, (1, cols), 1)

    def after(v):
        return jnp.where(lane == 0, 0.0, pltpu.roll(v, 1, 1))

    def ahead(v):
        return jnp.where(lane == cols - 1, 0.0, pltpu.roll(v, cols - 1, 1))

    def encode_one(t, scale=None):
        h = silu(dot(w1_ref[...], x1s[pl.ds(pl.multiple_of(96 * t, 16), 144), :]))
        if scale is not None:
            h = h * scale
        even, odd = h[:64], h[64:]
        base = pl.multiple_of(256 * t, 256)
        h1s[pl.ds(base, 64), :] = after(odd).astype(BF16)
        h1s[pl.ds(base + 64, 64), :] = even.astype(BF16)
        h1s[pl.ds(base + 128, 64), :] = odd.astype(BF16)
        h1s[pl.ds(base + 192, 64), :] = ahead(even).astype(BF16)

    def encode_two(t, scale=None):
        h = silu(dot(w2_ref[...], h1s[pl.ds(pl.multiple_of(256 * t, 256), 768), :]))
        if scale is not None:
            h = h * scale
        even, odd = h[:64], h[64:]
        base = pl.multiple_of(192 * t, 64)
        h2s[pl.ds(base, 64), :] = after(odd).astype(BF16)
        h2s[pl.ds(base + 64, 64), :] = even.astype(BF16)
        h2s[pl.ds(base + 128, 64), :] = odd.astype(BF16)

    def send(i, d):
        return pltpu.make_async_remote_copy(
            snd.at[i, d], rcv.at[i, pl.ds(pl.multiple_of(me * 16, 16), 16), :],
            a2a_send.at[i], a2a_recv.at[i], device_id={"mem": d}, device_id_type=MESH,
        )

    def encode_three(i):
        b = silu(dot(w3_ref[...], h2s[pl.ds(pl.multiple_of(384 * i, 64), 576), :]))
        padded = jnp.concatenate([b, jnp.zeros((16, 128), F32)], axis=1)
        for first, by in ((0, EDGE), (1, cols + 128 - (BLOCK - EDGE))):
            moved = pltpu.roll(padded, by, 1).astype(BF16)
            for d in range(first, nm, 2):
                start = BLOCK * (d - first)
                snd[i, d] = moved[:, start : start + 128]
        rcv[i, pl.ds(pl.multiple_of(me * 16, 16), 16), :] = snd[i, me]

        @pl.loop(1, nm)
        def _(step):
            send(i, lax.rem(me + step, nm)).start()

    @pl.loop(0, 10)
    def _(t):
        encode_one(t)

    encode_one(10, has_below)
    encode_two(0, has_above)

    @pl.loop(0, 4)
    def _(i):
        encode_two(2 * i + 1)
        encode_two(2 * i + 2)
        encode_three(i)

    def turn(v, by):
        return pltpu.roll(v, by % 128, 1)

    def keep_latent(i, v):
        base = 96 * (i + 2)
        latx[base : base + 32, :] = turn(v, 1).astype(BF16)
        latx[base + 32 : base + 64, :] = v.astype(BF16)
        latx[base + 64 : base + 96, :] = turn(v, -1).astype(BF16)

    latx[0:96, :] = jnp.zeros((96, 128), BF16)
    latx[672:768, :] = jnp.zeros((96, 128), BF16)

    for i in range(4):
        pltpu.make_async_copy(snd.at[i, pl.ds(0, nm - 1)], snd.at[i, pl.ds(0, nm - 1)], a2a_send.at[i]).wait()
    hops = []
    for i in (0, 3, 1, 2):
        landed = rcv.at[i, pl.ds(0, 16 * (nm - 1)), :]
        pltpu.make_async_copy(landed, landed, a2a_recv.at[i]).wait()
        v = silu(dot(mix_ref[...], rcv[i]))
        if i in (0, 3):
            side = 0 if i == 0 else 1
            lats[side] = v.astype(BF16)
            hop = pltpu.make_async_remote_copy(
                lats.at[side], lath.at[side], lat_send.at[side], lat_recv.at[side],
                device_id={"row": above if i == 0 else below}, device_id_type=MESH,
            )
            hop.start()
            hops.append(hop)
        keep_latent(i, v)
    for hop in hops:
        hop.wait()
    keep_latent(4, lath[0].astype(F32) * has_below)
    keep_latent(-1, lath[1].astype(F32) * has_above)

    place = me * BLOCK - EDGE + lane128
    inside = jnp.where((place >= 0) & (place < cols), 1.0, 0.0)
    for step in range(6):
        v = silu(dot(d1_ref[...], latx[96 * step : 96 * step + 288, :])) * inside
        if step == 0:
            v = v * has_above
        if step == 5:
            v = v * has_below
        for a in range(2):
            index = 2 * step - 1 + a
            if not 0 <= index < 10:
                continue
            even, odd = v[64 * a : 64 * a + 32], v[64 * a + 32 : 64 * a + 64]
            base = 128 * index
            upx[base : base + 32, :] = turn(odd, 1).astype(BF16)
            upx[base + 32 : base + 64, :] = even.astype(BF16)
            upx[base + 64 : base + 96, :] = odd.astype(BF16)
            upx[base + 96 : base + 128, :] = turn(even, -1).astype(BF16)
    for step in range(8):
        v = dot(d2_ref[...], upx[128 * step : 128 * step + 384, :]).astype(BF16)
        for a in range(2):
            for q in range(4):
                zz[16 * (2 * step + a) : 16 * (2 * step + a + 1), 128 * q : 128 * (q + 1)] = v[
                    16 * (4 * a + q) : 16 * (4 * a + q + 1)
                ]
    woven = dot(zz[...], one_hot((512, 256), lambda a, b: b == 4 * (a % 128 - EDGE) + a // 128))
    order = one_hot((256, 256), lambda a, b: b == (a % 16) * 16 + a // 16)
    out_ref[...] = dot(order, woven.astype(BF16)).astype(BF16).reshape(16, 16, 256)


def weights(enc_first, enc_second, enc_third, dec_first, dec_second):
    def join(pick, outs, taps, like):
        zero = jnp.zeros_like(like)
        return jnp.concatenate(
            [jnp.concatenate([pick(o, t) if pick(o, t) is not None else zero for t in taps], axis=1) for o in outs],
            axis=0,
        )

    one = jnp.pad(jnp.transpose(enc_first, (2, 3, 0, 1)), ((0, 0), (0, 0), (0, 0), (0, 3)))
    tap_one = {(0, 4): 0, (0, 0): 1, (0, 1): 2, (1, 1): 0, (1, 2): 1, (1, 3): 2}
    w1 = join(
        lambda b, t: one[t[0], tap_one[b, t[1]]] if (b, t[1]) in tap_one else None,
        range(2), [(u, v) for u in range(3) for v in range(6)], one[0, 0],
    )
    two = jnp.transpose(enc_second, (2, 3, 0, 1))
    w2 = join(
        lambda b, t: two[t[0], t[1] - b] if 0 <= t[1] - b < 3 else None,
        range(2), [(u, v) for u in range(3) for v in range(4)], two[0, 0],
    )
    three = jnp.transpose(enc_third, (2, 3, 0, 1))
    w3 = join(lambda _, t: three[t], range(1), [(u, v) for u in range(3) for v in range(3)], three[0, 0])
    grow = {(0, 0): 0, (0, 1): 2, (1, 1): 1, (1, 2): 3}
    first = jnp.transpose(dec_first, (2, 3, 0, 1))
    d1 = join(
        lambda o, t: first[grow[o[0], t[0]], grow[o[1], t[1]]]
        if (o[0], t[0]) in grow and (o[1], t[1]) in grow else None,
        [(a, b) for a in range(2) for b in range(2)],
        [(u, v) for u in range(3) for v in range(3)], first[0, 0],
    )
    second = jnp.transpose(dec_second, (2, 3, 0, 1))
    d2 = join(
        lambda o, t: second[grow[o[0], t[0]], grow[o[1] % 2, t[1] - o[1] // 2]]
        if (o[0], t[0]) in grow and (o[1] % 2, t[1] - o[1] // 2) in grow else None,
        [(a, q) for a in range(2) for q in range(4)],
        [(u, v) for u in range(3) for v in range(4)], second[0, 0],
    )
    return w1, w2, w3, d1, d2


def solution(mesh):
    nm, nr = mesh.shape["mem"], mesh.shape["row"]

    def per_device(members, enc_first, enc_second, enc_third, mix_weight, dec_first, dec_second):
        w1, w2, w3, d1, d2 = weights(enc_first, enc_second, enc_third, dec_first, dec_second)
        cols = nm * BLOCK
        dma = pltpu.SemaphoreType.DMA

        def body(*refs):
            kernel(nm, nr, *refs)

        return pl.pallas_call(
            body,
            out_shape=jax.ShapeDtypeStruct((16, 16, 4 * BLOCK), BF16),
            in_specs=[pl.BlockSpec(memory_space=pltpu.VMEM)] * 7,
            out_specs=pl.BlockSpec(memory_space=pltpu.VMEM),
            scratch_shapes=[
                pltpu.VMEM((5, 8, 4 * cols), BF16),
                pltpu.VMEM((5, 8, 4 * cols), BF16),
                pltpu.VMEM((23 * 48, cols), BF16),
                pltpu.VMEM((11 * 256, cols), BF16),
                pltpu.VMEM((9 * 192, cols), BF16),
                pltpu.VMEM((4, nm, 16, 128), BF16),
                pltpu.VMEM((4, nm * 16, 128), BF16),
                pltpu.VMEM((768, 128), BF16),
                pltpu.VMEM((2, 32, 128), BF16),
                pltpu.VMEM((2, 32, 128), BF16),
                pltpu.VMEM((1280, 128), BF16),
                pltpu.VMEM((256, 512), BF16),
                dma((2,)), dma((2,)), dma((4,)), dma((4,)), dma((2,)), dma((2,)),
            ],
            compiler_params=pltpu.CompilerParams(
                collective_id=0, has_side_effects=True, vmem_limit_bytes=60 * 1024 * 1024
            ),
        )(members[0], w1, w2, w3, mix_weight, d1, d2)

    placed = (P("mem", None, "row", None), P(), P(), P(), P(), P(), P())
    return jax.shard_map(
        per_device, mesh=mesh, in_specs=placed, out_specs=P(None, "row", "mem"), check_vma=False
    )
```

profile of v0, /device:TPU:1, one launch (start us, length us, event | category | flops | bytes accessed | tf_op | source)
XLA Modules:
  0.0 53.9 jit_solution(5291156956652622624)
XLA Ops:
  0.0 0.8 %slice_bitcast_fusion.50 = (bf16[16,64]{1,0:T(8,128)(2,1)S(1)}, bf16[16,64]{1,0:T(8,128)(2,1)S(1)}, bf16[16,64]{1,0:T(8,128)(2,1)S(1)}, bf16[16,64]{1,0:T(8,128)...) fusion(bf16[3,3,16,64]{3,2,1,0:T(8,128)(2,1)} %bitcast.133), kind=kLoop, calls=%fused_computation.63 | loop fusion | bytes 36864 | tf_op jit(solution)/shard_map/squeeze | solution.py:247
  0.8 0.7 %concatenate.69.refs_3_ = bf16[16,576]{1,0:T(8,128)(2,1)} concatenate(bf16[16,64]{1,0:T(8,128)(2,1)S(1)} %get-tuple-element.63, bf16[16,64]{1,0:T(8,128)(2,1)S(1)} %get-tuple-element.62, bf16[16,64]{1,0:T(8,128)(2,1)S(1)} %get-tuple-element.61, bf16[16,64]{1,0:T(8,128)(2,1)S(1)} %get-tuple-element.60, bf16[16,64]{1,0:T(8,128)(2,1)S(1)} %get-tuple-element.59, ...), dimensions={1} | concatenate | bytes 36864 | tf_op jit(solution)/shard_map/concatenate | solution.py:231
  1.6 0.1 concatenate.82
  1.7 0.1 concatenate.80
  1.9 0.1 concatenate.77
  2.0 0.1 concatenate.81
  2.1 0.1 concatenate.79
  2.2 0.1 concatenate.76
  2.5 0.6 %copy-done.1 = bf16[32,32,4,4]{1,3,2,0:T(4,128)(2,1)S(1)} copy-done((bf16[32,32,4,4]{1,3,2,0:T(4,128)(2,1)S(1)}, bf16[32,32,4,4]{1,3,2,0:T(4,128)(2,1)}, u32[]{:S(2)}) %copy-start.1) | copy-done | bytes 32792
  3.1 0.6 %copy-done.2 = bf16[128,384]{1,0:T(8,128)(2,1)} copy-done((bf16[128,384]{1,0:T(8,128)(2,1)}, bf16[128,384]{1,0:T(8,128)(2,1)S(1)}, u32[]{:S(2)}) %copy-start.2) | copy-done | bytes 98328
  3.8 0.1 concatenate.70
  4.0 0.1 concatenate.72
  4.1 0.1 concatenate.71
  4.2 0.7 %pad_maximum_fusion.1.refs_5_ = bf16[128,288]{1,0:T(8,128)(2,1)} fusion(bf16[32,288]{1,0:T(8,128)(2,1)S(1)} %concatenate.73, bf16[32,288]{1,0:T(8,128)(2,1)S(1)} %concatenate.72, bf16[32,288]{1,0:T(8,128)(2,1)S(1)} %concatenate.71, bf16[32,288]{1,0:T(8,128)(2,1)S(1)} %concatenate.70), kind=kLoop, calls=%fused_computation.2 | loop fusion | flops 294912 | bytes 147456 | tf_op jit(solution)/shard_map/concatenate | solution.py:230
  4.9 0.2 copy.8
  5.2 0.1 concatenate.64
  5.3 0.1 concatenate.63
  5.5 0.6 %pad_maximum_fusion.2.refs_1_ = bf16[128,144]{1,0:T(8,128)(2,1)} fusion(bf16[64,144]{1,0:T(8,128)(2,1)S(1)} %concatenate.64, bf16[64,144]{1,0:T(8,128)(2,1)S(1)} %concatenate.63), kind=kLoop, calls=%fused_computation.3 | loop fusion | flops 73728 | bytes 73728 | tf_op jit(solution)/shard_map/concatenate | solution.py:230
  6.1 0.1 copy-done
  6.2 0.1 concatenate.67
  6.4 0.1 concatenate.66
  6.5 0.7 %pad_maximum_fusion.refs_2_ = bf16[128,768]{1,0:T(8,128)(2,1)} fusion(bf16[64,768]{1,0:T(8,128)(2,1)S(1)} %concatenate.67, bf16[64,768]{1,0:T(8,128)(2,1)S(1)} %concatenate.66), kind=kLoop, calls=%fused_computation | loop fusion | flops 393216 | bytes 393216 | tf_op jit(solution)/shard_map/concatenate | solution.py:230
  7.2 45.2 %shard_map.73 = bf16[16,16,256]{2,1,0:T(8,128)(2,1)} custom-call(bf16[5,16,4096]{2,1,0:T(8,128)(2,1)} %bitcast.128, bf16[128,144]{1,0:T(8,128)(2,1)} %pad_maximum_fusion.2.refs_1_, bf16[128,768]{1,0:T(8,128)(2,1)} %pad_maximum_fusion.refs_2_, bf16[16,576]{1,0:T(8,128)(2,1)} %concatenate.69.refs_3_, bf16[32,256]{1,0:T(8,128)(2,1)} %refs_4_.1, ...), custom_call_target="tpu_custom_call" | custom-call | tf_op jit(solution)/shard_map/pallas_call | solution.py:277
  52.3 1.6 %copy.23 = bf16[16,16,256]{2,1,0:T(8,128)(2,1)} copy(bf16[16,16,256]{2,1,0:T(8,128)(2,1)} %shard_map.73) | data formatting | bytes 262144
  (36 shorter events, 0.6 us)
Async XLA Ops:
  0.0 1.5 %copy-start.3 = (bf16[16,32,4,4]{1,3,2,0:T(4,128)(2,1)S(1)}, bf16[16,32,4,4]{1,3,2,0:T(4,128)(2,1)}, u32[]{:S(2)}) copy-start(bf16[16,32,4,4]{1,3,2,0:T(4,128)(2,1)} %param.13) | copy-start | bytes 49156
  2.2 0.9 %copy-start.1 = (bf16[32,32,4,4]{1,3,2,0:T(4,128)(2,1)S(1)}, bf16[32,32,4,4]{1,3,2,0:T(4,128)(2,1)}, u32[]{:S(2)}) copy-start(bf16[32,32,4,4]{1,3,2,0:T(4,128)(2,1)} %param.12) | copy-start | bytes 98308
  3.1 0.6 %copy-start.2 = (bf16[128,384]{1,0:T(8,128)(2,1)}, bf16[128,384]{1,0:T(8,128)(2,1)S(1)}, u32[]{:S(2)}) copy-start(bf16[128,384]{1,0:T(8,128)(2,1)S(1)} %constant_dynamic-update-slice_fusion.refs_6_) | copy-start | bytes 294916
  4.2 0.7 %copy-start.4 = (bf16[64,5,3,3]{0,3,2,1:T(4,128)(2,1)S(1)}, bf16[64,5,3,3]{0,3,2,1:T(4,128)(2,1)}, u32[]{:S(2)}) copy-start(bf16[64,5,3,3]{0,3,2,1:T(4,128)(2,1)} %param.8) | copy-start | bytes 17284
  5.3 0.9 %copy-start = (bf16[64,64,3,3]{1,0,3,2:T(8,128)(2,1)S(1)}, bf16[64,64,3,3]{1,0,3,2:T(8,128)(2,1)}, u32[]{:S(2)}) copy-start(bf16[64,64,3,3]{1,0,3,2:T(8,128)(2,1)} %param.9) | copy-start | bytes 221188
where the time goes:
time: 54.2 us; the launch traced here: 53.9 us
  Pallas kernels  45.2 us (83%)
  local copies, waits for them, and re-layouts  6.58 us (12%)
  other arithmetic  1.97 us (4%)
    pallas_call x1, Pallas kernels, per_device(): pl.pallas_call(body, out_shape=jax.ShapeDtypeStruct((16, 16, 4 * BLOCK),...  45.2 us
    unnamed x21, local copies, waits for them, and re-layouts  3.24 us
    concatenate x17, local copies, waits for them, and re-layouts, join(): jnp.concatenate([pick(o, t) if pick(o, t) is not None else zero for t in...  2.38 us
    concatenate x3, other arithmetic, join(): jnp.concatenate([jnp.concatenate([pick(o, t) if pick(o, t) is not None el...  1.97 us

commit v1 on v0

--- a/solution.py
+++ b/solution.py
@@ -65,67 +65,69 @@
 
     phases = one_hot((512, 512), lambda a, b: a == 4 * (b % 128) + b // 128)
     lane128 = lax.broadcasted_iota(jnp.int32, (1, 128), 1)
-
-    def split(source, select, first, count, scale):
-        flat = source.reshape(source.shape[0] * source.shape[1], source.shape[2])
-        before = jnp.zeros((select.shape[0], 128), F32)
+    chunks = cols // 128
+
+    def split(flat, select, slots, scale):
+        ordered = dot(select, flat)
+        if scale is not None:
+            ordered = ordered * scale
+        ordered = ordered.astype(BF16)
+        high = select.shape[0]
+        stack = jnp.concatenate([ordered[:, 512 * k : 512 * (k + 1)] for k in range(chunks)], axis=0)
+        first = dot(stack, phases[:, :256])
+        last = dot(stack, phases[:, 256:])
         zero = jnp.zeros((8, 128), F32)
-        for k in range(cols // 128):
-            ordered = dot(select, flat[:, 512 * k : 512 * (k + 1)])
-            if scale is not None:
-                ordered = ordered * scale
-            z = dot(ordered.astype(BF16), phases)
-            turned = pltpu.roll(z[:, 384:512], 1, 1)
-            late = jnp.where(lane128 == 0, before, turned)
-            before = turned
-            for r in range(count):
-                part = slice(8 * r, 8 * r + 8)
-                tile = jnp.concatenate(
-                    [z[part, 0:128], z[part, 128:256], z[part, 256:384], z[part, 384:512],
-                     late[part], zero],
-                    axis=0,
-                )
-                x1s[48 * (first + r) : 48 * (first + r + 1), 128 * k : 128 * (k + 1)] = (
-                    tile.astype(BF16)
-                )
-
-    split(x_ref[...], one_hot((128, 80), lambda a, b: (a % 8 < 5) & (b == (a % 8) * 16 + a // 8)),
-          5, 16, None)
-    down.wait()
-    up.wait()
-    split(top[...], one_hot((48, 40), lambda a, b: (a % 8 < 5) & (a < 40) & (b == (a % 8) * 8 + 3 + a // 8)),
-          0, 5, has_above)
-    split(bot[...], one_hot((16, 40), lambda a, b: (a % 8 < 5) & (b == (a % 8) * 8 + a // 8)),
-          21, 2, has_below)
+        for r, slot in enumerate(slots):
+            before = jnp.zeros((8, 128), F32)
+            for k in range(chunks):
+                part = slice(high * k + 8 * r, high * k + 8 * r + 8)
+                turned = pltpu.roll(last[part, 128:256], 1, 1)
+                late = jnp.where(lane128 == 0, before, turned)
+                before = turned
+                for base, upper, lower in (
+                    (0, first[part, 0:128], first[part, 128:256]),
+                    (16, last[part, 0:128], last[part, 128:256]),
+                    (32, late, zero),
+                ):
+                    x1s[48 * slot + base : 48 * slot + base + 16, 128 * k : 128 * (k + 1)] = (
+                        jnp.concatenate([upper, lower], axis=0).astype(BF16)
+                    )
+
+    split(x_ref[...].reshape(80, 4 * cols),
+          one_hot((128, 80), lambda a, b: (a % 8 < 5) & (b == (a % 8) * 16 + a // 8)),
+          range(5, 21), None)
 
     lane = lax.broadcasted_iota(jnp.int32, (1, cols), 1)
 
+    not_first = jnp.where(lane == 0, 0.0, 1.0).astype(BF16)
+    not_last = jnp.where(lane == cols - 1, 0.0, 1.0).astype(BF16)
+
     def after(v):
-        return jnp.where(lane == 0, 0.0, pltpu.roll(v, 1, 1))
+        return pltpu.roll(v, 1, 1) * not_first
 
     def ahead(v):
-        return jnp.where(lane == cols - 1, 0.0, pltpu.roll(v, cols - 1, 1))
+        return pltpu.roll(v, cols - 1, 1) * not_last
 
     def encode_one(t, scale=None):
-        h = silu(dot(w1_ref[...], x1s[pl.ds(pl.multiple_of(96 * t, 16), 144), :]))
+        h = silu(dot(w1_ref[...], x1s[pl.ds(pl.multiple_of(96 * t, 16), 144), :]).astype(BF16))
         if scale is not None:
-            h = h * scale
+            h = h * scale.astype(BF16)
         even, odd = h[:64], h[64:]
         base = pl.multiple_of(256 * t, 256)
-        h1s[pl.ds(base, 64), :] = after(odd).astype(BF16)
-        h1s[pl.ds(base + 64, 64), :] = even.astype(BF16)
-        h1s[pl.ds(base + 128, 64), :] = odd.astype(BF16)
-        h1s[pl.ds(base + 192, 64), :] = ahead(even).astype(BF16)
+        h1s[pl.ds(base, 64), :] = after(odd)
+        h1s[pl.ds(base + 64, 64), :] = even
+        h1s[pl.ds(base + 128, 64), :] = odd
+        h1s[pl.ds(base + 192, 64), :] = ahead(even)
 
     def encode_two(t, scale=None):
-        h = silu(dot(w2_ref[...], h1s[pl.ds(pl.multiple_of(256 * t, 256), 768), :]))
+        h = silu(dot(w2_ref[...], h1s[pl.ds(pl.multiple_of(256 * t, 256), 768), :]).astype(BF16))
         if scale is not None:
-            h = h * scale
+            h = h * scale.astype(BF16)
         even, odd = h[:64], h[64:]
         base = pl.multiple_of(192 * t, 64)
-        h2s[pl.ds(base, 64), :] = after(odd).astype(BF16)
-        h2s[pl.ds(base + 64, 64), :] = even.astype(BF16)
-        h2s[pl.ds(base + 128, 64), :] = odd.astype(BF16)
+        h2s[pl.ds(base, 64), :] = after(odd)
+        h2s[pl.ds(base + 64, 64), :] = even
+        h2s[pl.ds(base + 128, 64), :] = odd
 
     def send(i, d):
         return pltpu.make_async_remote_copy(
@@ -147,7 +149,24 @@
         def _(step):
             send(i, lax.rem(me + step, nm)).start()
 
-    @pl.loop(0, 10)
+    @pl.loop(3, 10)
+    def _(t):
+        encode_one(t)
+
+    down.wait()
+    up.wait()
+    edge = lax.broadcasted_iota(jnp.int32, (64, 1), 0)
+    split(
+        jnp.concatenate([top[...].reshape(40, 4 * cols), bot[...].reshape(40, 4 * cols)], axis=0),
+        one_hot(
+            (64, 80),
+            lambda a, b: (a % 8 < 5) & (a < 56)
+            & (b == (a % 8) * 8 + jnp.where(a < 40, 3 + a // 8, 35 + a // 8)),
+        ),
+        (0, 1, 2, 3, 4, 21, 22), jnp.where(edge < 40, has_above, has_below),
+    )
+
+    @pl.loop(0, 3)
     def _(t):
         encode_one(t)
 

time: 54.2 us -> 48.6 us (0.90)
  Pallas kernels: 45.2 us -> 39.6 us
    pallas_call x1, Pallas kernels: 45.2 us -> 39.6 us  [per_device(): pl.pallas_call(body, out_shape=jax.ShapeDtypeStruct((16, 16, 4 * BLOCK),...]
where the time goes in v1:
time: 48.6 us; the launch traced here: 48.4 us
  Pallas kernels  39.6 us (81%)
  local copies, waits for them, and re-layouts  6.58 us (14%)
  other arithmetic  1.97 us (4%)
    pallas_call x1, Pallas kernels, per_device(): pl.pallas_call(body, out_shape=jax.ShapeDtypeStruct((16, 16, 4 * BLOCK),...  39.6 us
    unnamed x21, local copies, waits for them, and re-layouts  3.24 us
    concatenate x17, local copies, waits for them, and re-layouts, join(): jnp.concatenate([pick(o, t) if pick(o, t) is not None else zero for t in...  2.38 us
    concatenate x3, other arithmetic, join(): jnp.concatenate([jnp.concatenate([pick(o, t) if pick(o, t) is not None el...  1.97 us

profile of v1, /device:TPU:1, one launch (start us, length us, event | category | flops | bytes accessed | tf_op | source)
XLA Modules:
  0.0 48.4 jit_solution(4767589169967776550)
XLA Ops:
  0.0 0.8 %slice_bitcast_fusion.50 = (bf16[16,64]{1,0:T(8,128)(2,1)S(1)}, bf16[16,64]{1,0:T(8,128)(2,1)S(1)}, bf16[16,64]{1,0:T(8,128)(2,1)S(1)}, bf16[16,64]{1,0:T(8,128)...) fusion(bf16[3,3,16,64]{3,2,1,0:T(8,128)(2,1)} %bitcast.133), kind=kLoop, calls=%fused_computation.63 | loop fusion | bytes 36864 | tf_op jit(solution)/shard_map/squeeze | solution.py:266
  0.8 0.7 %concatenate.69.refs_3_ = bf16[16,576]{1,0:T(8,128)(2,1)} concatenate(bf16[16,64]{1,0:T(8,128)(2,1)S(1)} %get-tuple-element.63, bf16[16,64]{1,0:T(8,128)(2,1)S(1)} %get-tuple-element.62, bf16[16,64]{1,0:T(8,128)(2,1)S(1)} %get-tuple-element.61, bf16[16,64]{1,0:T(8,128)(2,1)S(1)} %get-tuple-element.60, bf16[16,64]{1,0:T(8,128)(2,1)S(1)} %get-tuple-element.59, ...), dimensions={1} | concatenate | bytes 36864 | tf_op jit(solution)/shard_map/concatenate | solution.py:250
  1.6 0.1 concatenate.82
  1.7 0.1 concatenate.80
  1.9 0.1 concatenate.77
  2.0 0.1 concatenate.81
  2.1 0.1 concatenate.79
  2.2 0.1 concatenate.76
  2.5 0.6 %copy-done.1 = bf16[32,32,4,4]{1,3,2,0:T(4,128)(2,1)S(1)} copy-done((bf16[32,32,4,4]{1,3,2,0:T(4,128)(2,1)S(1)}, bf16[32,32,4,4]{1,3,2,0:T(4,128)(2,1)}, u32[]{:S(2)}) %copy-start.1) | copy-done | bytes 32792
  3.1 0.6 %copy-done.2 = bf16[128,384]{1,0:T(8,128)(2,1)} copy-done((bf16[128,384]{1,0:T(8,128)(2,1)}, bf16[128,384]{1,0:T(8,128)(2,1)S(1)}, u32[]{:S(2)}) %copy-start.2) | copy-done | bytes 98328
  3.8 0.1 concatenate.70
  4.0 0.1 concatenate.72
  4.1 0.1 concatenate.71
  4.2 0.7 %pad_maximum_fusion.1.refs_5_ = bf16[128,288]{1,0:T(8,128)(2,1)} fusion(bf16[32,288]{1,0:T(8,128)(2,1)S(1)} %concatenate.73, bf16[32,288]{1,0:T(8,128)(2,1)S(1)} %concatenate.72, bf16[32,288]{1,0:T(8,128)(2,1)S(1)} %concatenate.71, bf16[32,288]{1,0:T(8,128)(2,1)S(1)} %concatenate.70), kind=kLoop, calls=%fused_computation.2 | loop fusion | flops 294912 | bytes 147456 | tf_op jit(solution)/shard_map/concatenate | solution.py:249
  4.9 0.2 copy.8
  5.2 0.1 concatenate.64
  5.3 0.1 concatenate.63
  5.5 0.6 %pad_maximum_fusion.2.refs_1_ = bf16[128,144]{1,0:T(8,128)(2,1)} fusion(bf16[64,144]{1,0:T(8,128)(2,1)S(1)} %concatenate.64, bf16[64,144]{1,0:T(8,128)(2,1)S(1)} %concatenate.63), kind=kLoop, calls=%fused_computation.3 | loop fusion | flops 73728 | bytes 73728 | tf_op jit(solution)/shard_map/concatenate | solution.py:249
  6.1 0.1 copy-done
  6.2 0.1 concatenate.67
  6.4 0.1 concatenate.66
  6.5 0.7 %pad_maximum_fusion.refs_2_ = bf16[128,768]{1,0:T(8,128)(2,1)} fusion(bf16[64,768]{1,0:T(8,128)(2,1)S(1)} %concatenate.67, bf16[64,768]{1,0:T(8,128)(2,1)S(1)} %concatenate.66), kind=kLoop, calls=%fused_computation | loop fusion | flops 393216 | bytes 393216 | tf_op jit(solution)/shard_map/concatenate | solution.py:249
  7.2 39.6 %shard_map.73 = bf16[16,16,256]{2,1,0:T(8,128)(2,1)} custom-call(bf16[5,16,4096]{2,1,0:T(8,128)(2,1)} %bitcast.128, bf16[128,144]{1,0:T(8,128)(2,1)} %pad_maximum_fusion.2.refs_1_, bf16[128,768]{1,0:T(8,128)(2,1)} %pad_maximum_fusion.refs_2_, bf16[16,576]{1,0:T(8,128)(2,1)} %concatenate.69.refs_3_, bf16[32,256]{1,0:T(8,128)(2,1)} %refs_4_.1, ...), custom_call_target="tpu_custom_call" | custom-call | tf_op jit(solution)/shard_map/pallas_call | solution.py:296
  46.8 1.6 %copy.23 = bf16[16,16,256]{2,1,0:T(8,128)(2,1)} copy(bf16[16,16,256]{2,1,0:T(8,128)(2,1)} %shard_map.73) | data formatting | bytes 262144
  (36 shorter events, 0.6 us)
Async XLA Ops:
  0.0 1.5 %copy-start.3 = (bf16[16,32,4,4]{1,3,2,0:T(4,128)(2,1)S(1)}, bf16[16,32,4,4]{1,3,2,0:T(4,128)(2,1)}, u32[]{:S(2)}) copy-start(bf16[16,32,4,4]{1,3,2,0:T(4,128)(2,1)} %param.13) | copy-start | bytes 49156
  2.2 0.9 %copy-start.1 = (bf16[32,32,4,4]{1,3,2,0:T(4,128)(2,1)S(1)}, bf16[32,32,4,4]{1,3,2,0:T(4,128)(2,1)}, u32[]{:S(2)}) copy-start(bf16[32,32,4,4]{1,3,2,0:T(4,128)(2,1)} %param.12) | copy-start | bytes 98308
  3.1 0.6 %copy-start.2 = (bf16[128,384]{1,0:T(8,128)(2,1)}, bf16[128,384]{1,0:T(8,128)(2,1)S(1)}, u32[]{:S(2)}) copy-start(bf16[128,384]{1,0:T(8,128)(2,1)S(1)} %constant_dynamic-update-slice_fusion.refs_6_) | copy-start | bytes 294916
  4.2 0.7 %copy-start.4 = (bf16[64,5,3,3]{0,3,2,1:T(4,128)(2,1)S(1)}, bf16[64,5,3,3]{0,3,2,1:T(4,128)(2,1)}, u32[]{:S(2)}) copy-start(bf16[64,5,3,3]{0,3,2,1:T(4,128)(2,1)} %param.8) | copy-start | bytes 17284
  5.3 0.9 %copy-start = (bf16[64,64,3,3]{1,0,3,2:T(8,128)(2,1)S(1)}, bf16[64,64,3,3]{1,0,3,2:T(8,128)(2,1)}, u32[]{:S(2)}) copy-start(bf16[64,64,3,3]{1,0,3,2:T(8,128)(2,1)} %param.9) | copy-start | bytes 221188

commit v2 on v1

--- a/solution.py
+++ b/solution.py
@@ -28,8 +28,8 @@
 
 
 def kernel(
-    nm, nr, x_ref, w1_ref, w2_ref, w3_ref, mix_ref, d1_ref, d2_ref, out_ref,
-    top, bot, x1s, h1s, h2s, snd, rcv, latx, lats, lath, upx, zz,
+    nm, nr, x_ref, first_ref, second_ref, third_ref, mix_ref, grow_one_ref, grow_two_ref, out_ref,
+    w1_ref, w2_ref, w3_ref, d1_ref, d2_ref, top, bot, x1s, h1s, h2s, snd, rcv, latx, lats, lath, upx, zz,
     halo_send, halo_recv, a2a_send, a2a_recv, lat_send, lat_recv,
 ):
     me = lax.axis_index("mem")
@@ -47,6 +47,10 @@
             barrier, inc=1, device_id={"mem": lax.rem(me + step, nm)}, device_id_type=MESH
         )
 
+    weights(
+        first_ref, second_ref, third_ref, grow_one_ref, grow_two_ref,
+        w1_ref, w2_ref, w3_ref, d1_ref, d2_ref,
+    )
     pl.semaphore_wait(barrier, nm + 1)
 
     down = pltpu.make_async_remote_copy(
@@ -243,50 +247,64 @@
     out_ref[...] = dot(order, woven.astype(BF16)).astype(BF16).reshape(16, 16, 256)
 
 
-def weights(enc_first, enc_second, enc_third, dec_first, dec_second):
-    def join(pick, outs, taps, like):
-        zero = jnp.zeros_like(like)
-        return jnp.concatenate(
-            [jnp.concatenate([pick(o, t) if pick(o, t) is not None else zero for t in taps], axis=1) for o in outs],
-            axis=0,
+def weights(first, second, third, grow_one, grow_two, w1, w2, w3, d1, d2):
+    def across(blocks, like):
+        return jnp.concatenate([jnp.zeros_like(like) if v is None else v for v in blocks], axis=1)
+
+    tap_one = {(0, 4): 0, (0, 0): 1, (0, 1): 2, (1, 1): 0, (1, 2): 1, (1, 3): 2}
+    pad = jnp.zeros((3, 64), F32)
+    one = [
+        [jnp.concatenate([first[:, u, k, :].astype(F32), pad], axis=0) for k in range(3)]
+        for u in range(3)
+    ]
+    turned = jnp.concatenate(
+        [
+            across([one[u][tap_one[b, v]] if (b, v) in tap_one else None for b in range(2)], one[0][0])
+            for u in range(3) for v in range(6)
+        ],
+        axis=0,
+    ).astype(BF16)
+    same = one_hot((128, 128), lambda a, b: a == b)
+    w1[...] = lax.dot_general(
+        same, turned, (((1,), (1,)), ((), ())), preferred_element_type=F32
+    ).astype(BF16)
+
+    two = [[second[u, k] for k in range(3)] for u in range(3)]
+    for b in range(2):
+        w2[64 * b : 64 * b + 64, :] = across(
+            [two[u][v - b] if 0 <= v - b < 3 else None for u in range(3) for v in range(4)], two[0][0]
         )
-
-    one = jnp.pad(jnp.transpose(enc_first, (2, 3, 0, 1)), ((0, 0), (0, 0), (0, 0), (0, 3)))
-    tap_one = {(0, 4): 0, (0, 0): 1, (0, 1): 2, (1, 1): 0, (1, 2): 1, (1, 3): 2}
-    w1 = join(
-        lambda b, t: one[t[0], tap_one[b, t[1]]] if (b, t[1]) in tap_one else None,
-        range(2), [(u, v) for u in range(3) for v in range(6)], one[0, 0],
-    )
-    two = jnp.transpose(enc_second, (2, 3, 0, 1))
-    w2 = join(
-        lambda b, t: two[t[0], t[1] - b] if 0 <= t[1] - b < 3 else None,
-        range(2), [(u, v) for u in range(3) for v in range(4)], two[0, 0],
-    )
-    three = jnp.transpose(enc_third, (2, 3, 0, 1))
-    w3 = join(lambda _, t: three[t], range(1), [(u, v) for u in range(3) for v in range(3)], three[0, 0])
+    three = [third[u, v] for u in range(3) for v in range(3)]
+    w3[...] = across(three, three[0])
+
     grow = {(0, 0): 0, (0, 1): 2, (1, 1): 1, (1, 2): 3}
-    first = jnp.transpose(dec_first, (2, 3, 0, 1))
-    d1 = join(
-        lambda o, t: first[grow[o[0], t[0]], grow[o[1], t[1]]]
-        if (o[0], t[0]) in grow and (o[1], t[1]) in grow else None,
-        [(a, b) for a in range(2) for b in range(2)],
-        [(u, v) for u in range(3) for v in range(3)], first[0, 0],
-    )
-    second = jnp.transpose(dec_second, (2, 3, 0, 1))
-    d2 = join(
-        lambda o, t: second[grow[o[0], t[0]], grow[o[1] % 2, t[1] - o[1] // 2]]
-        if (o[0], t[0]) in grow and (o[1] % 2, t[1] - o[1] // 2) in grow else None,
-        [(a, q) for a in range(2) for q in range(4)],
-        [(u, v) for u in range(3) for v in range(4)], second[0, 0],
-    )
-    return w1, w2, w3, d1, d2
+    taps = [[grow_one[:, k, l, :] for l in range(4)] for k in range(4)]
+    for a in range(2):
+        for b in range(2):
+            d1[32 * (2 * a + b) : 32 * (2 * a + b) + 32, :] = across(
+                [
+                    taps[grow[a, u]][grow[b, v]] if (a, u) in grow and (b, v) in grow else None
+                    for u in range(3) for v in range(3)
+                ],
+                taps[0][0],
+            )
+    taps = [[grow_two[:, k, l, :] for l in range(4)] for k in range(4)]
+    for a in range(2):
+        for q in range(4):
+            d2[16 * (4 * a + q) : 16 * (4 * a + q) + 16, :] = across(
+                [
+                    taps[grow[a, u]][grow[q % 2, v - q // 2]]
+                    if (a, u) in grow and (q % 2, v - q // 2) in grow else None
+                    for u in range(3) for v in range(4)
+                ],
+                taps[0][0],
+            )
 
 
 def solution(mesh):
     nm, nr = mesh.shape["mem"], mesh.shape["row"]
 
     def per_device(members, enc_first, enc_second, enc_third, mix_weight, dec_first, dec_second):
-        w1, w2, w3, d1, d2 = weights(enc_first, enc_second, enc_third, dec_first, dec_second)
         cols = nm * BLOCK
         dma = pltpu.SemaphoreType.DMA
 
@@ -299,6 +317,11 @@
             in_specs=[pl.BlockSpec(memory_space=pltpu.VMEM)] * 7,
             out_specs=pl.BlockSpec(memory_space=pltpu.VMEM),
             scratch_shapes=[
+                pltpu.VMEM((128, 144), BF16),
+                pltpu.VMEM((128, 768), BF16),
+                pltpu.VMEM((16, 576), BF16),
+                pltpu.VMEM((128, 288), BF16),
+                pltpu.VMEM((128, 384), BF16),
                 pltpu.VMEM((5, 8, 4 * cols), BF16),
                 pltpu.VMEM((5, 8, 4 * cols), BF16),
                 pltpu.VMEM((23 * 48, cols), BF16),
@@ -316,7 +339,15 @@
             compiler_params=pltpu.CompilerParams(
                 collective_id=0, has_side_effects=True, vmem_limit_bytes=60 * 1024 * 1024
             ),
-        )(members[0], w1, w2, w3, mix_weight, d1, d2)
+        )(
+            members[0],
+            jnp.transpose(enc_first, (1, 2, 3, 0)),
+            jnp.transpose(enc_second, (2, 3, 0, 1)),
+            jnp.transpose(enc_third, (2, 3, 0, 1)),
+            mix_weight,
+            jnp.transpose(dec_first, (0, 2, 3, 1)),
+            jnp.transpose(dec_second, (0, 2, 3, 1)),
+        )
 
     placed = (P("mem", None, "row", None), P(), P(), P(), P(), P(), P())
     return jax.shard_map(

time: 48.6 us -> 41.5 us (0.85)
  local copies, waits for them, and re-layouts: 6.58 us -> 1.57 us
  other arithmetic: 1.97 us -> 0 us
    concatenate x18 -> x0, local copies, waits for them, and re-layouts: 2.39 us -> none  [the longest x17 2.38 us: join(): jnp.concatenate([pick(o, t) if pick(o, t) is not None else zero for t in...]
    concatenate x3 -> x0, other arithmetic: 1.97 us -> none  [join(): jnp.concatenate([jnp.concatenate([pick(o, t) if pick(o, t) is not None el...]
    unnamed x21 -> x1, local copies, waits for them, and re-layouts: 3.24 us -> 1.57 us
    squeeze x5 -> x0, local copies, waits for them, and re-layouts: 0.91 us -> none  [the longest x1 0.84 us: weights(): three[t]]
where the time goes in v2:
time: 41.5 us; the launch traced here: 41.4 us
  Pallas kernels  39.9 us (96%)
  local copies, waits for them, and re-layouts  1.57 us (4%)
    pallas_call x1, Pallas kernels, per_device(): pl.pallas_call(body, out_shape=jax.ShapeDtypeStruct((16, 16, 4 * BLOCK),...  39.9 us
    unnamed x1, local copies, waits for them, and re-layouts  1.57 us

profile of v2, /device:TPU:1, one launch (start us, length us, event | category | flops | bytes accessed | tf_op | source)
XLA Modules:
  0.0 41.4 jit_solution(18058678887620739930)
XLA Ops:
  0.0 39.9 %shard_map.73 = bf16[16,16,256]{2,1,0:T(8,128)(2,1)} custom-call(bf16[5,16,4096]{2,1,0:T(8,128)(2,1)} %bitcast.6, bf16[5,3,3,64]{3,2,1,0:T(4,128)(2,1)} %bitcast.11, bf16[3,3,64,64]{3,2,1,0:T(8,128)(2,1)} %bitcast.7, bf16[3,3,16,64]{3,2,1,0:T(8,128)(2,1)} %bitcast.10, bf16[32,256]{1,0:T(8,128)(2,1)} %refs_4_.1, bf16[32,4,4,32]{3,2,1,0:T(4,128)(2,1)} %bitcast.8, ...), custom_call_target="tpu_custom_call" | custom-call | tf_op jit(solution)/shard_map/pallas_call | solution.py:314
  39.9 1.6 %copy.9 = bf16[16,16,256]{2,1,0:T(8,128)(2,1)} copy(bf16[16,16,256]{2,1,0:T(8,128)(2,1)} %shard_map.73) | data formatting | bytes 262144

commit v3 on v2

--- a/solution.py
+++ b/solution.py
@@ -113,22 +113,22 @@
         return pltpu.roll(v, cols - 1, 1) * not_last
 
     def encode_one(t, scale=None):
-        h = silu(dot(w1_ref[...], x1s[pl.ds(pl.multiple_of(96 * t, 16), 144), :]).astype(BF16))
+        h = silu(dot(w1_ref[...], x1s[pl.ds(96 * t, 144), :]).astype(BF16))
         if scale is not None:
             h = h * scale.astype(BF16)
         even, odd = h[:64], h[64:]
-        base = pl.multiple_of(256 * t, 256)
+        base = 256 * t
         h1s[pl.ds(base, 64), :] = after(odd)
         h1s[pl.ds(base + 64, 64), :] = even
         h1s[pl.ds(base + 128, 64), :] = odd
         h1s[pl.ds(base + 192, 64), :] = ahead(even)
 
     def encode_two(t, scale=None):
-        h = silu(dot(w2_ref[...], h1s[pl.ds(pl.multiple_of(256 * t, 256), 768), :]).astype(BF16))
+        h = silu(dot(w2_ref[...], h1s[pl.ds(256 * t, 768), :]).astype(BF16))
         if scale is not None:
             h = h * scale.astype(BF16)
         even, odd = h[:64], h[64:]
-        base = pl.multiple_of(192 * t, 64)
+        base = 192 * t
         h2s[pl.ds(base, 64), :] = after(odd)
         h2s[pl.ds(base + 64, 64), :] = even
         h2s[pl.ds(base + 128, 64), :] = odd
@@ -140,7 +140,7 @@
         )
 
     def encode_three(i):
-        b = silu(dot(w3_ref[...], h2s[pl.ds(pl.multiple_of(384 * i, 64), 576), :]))
+        b = silu(dot(w3_ref[...], h2s[pl.ds(384 * i, 576), :]))
         padded = jnp.concatenate([b, jnp.zeros((16, 128), F32)], axis=1)
         for first, by in ((0, EDGE), (1, cols + 128 - (BLOCK - EDGE))):
             moved = pltpu.roll(padded, by, 1).astype(BF16)
@@ -149,13 +149,14 @@
                 snd[i, d] = moved[:, start : start + 128]
         rcv[i, pl.ds(pl.multiple_of(me * 16, 16), 16), :] = snd[i, me]
 
-        @pl.loop(1, nm)
-        def _(step):
+        for step in range(1, nm):
             send(i, lax.rem(me + step, nm)).start()
 
-    @pl.loop(3, 10)
-    def _(t):
+    for t in range(3, 10):
         encode_one(t)
+    for t in range(3, 8):
+        encode_two(t)
+    encode_three(2)
 
     down.wait()
     up.wait()
@@ -170,18 +171,16 @@
         (0, 1, 2, 3, 4, 21, 22), jnp.where(edge < 40, has_above, has_below),
     )
 
-    @pl.loop(0, 3)
-    def _(t):
+    encode_one(10, has_below)
+    encode_two(8)
+    encode_three(3)
+    for t in range(3):
         encode_one(t)
-
-    encode_one(10, has_below)
     encode_two(0, has_above)
-
-    @pl.loop(0, 4)
-    def _(i):
-        encode_two(2 * i + 1)
-        encode_two(2 * i + 2)
-        encode_three(i)
+    encode_two(1)
+    encode_two(2)
+    encode_three(0)
+    encode_three(1)
 
     def turn(v, by):
         return pltpu.roll(v, by % 128, 1)
@@ -195,10 +194,8 @@
     latx[0:96, :] = jnp.zeros((96, 128), BF16)
     latx[672:768, :] = jnp.zeros((96, 128), BF16)
 
-    for i in range(4):
-        pltpu.make_async_copy(snd.at[i, pl.ds(0, nm - 1)], snd.at[i, pl.ds(0, nm - 1)], a2a_send.at[i]).wait()
     hops = []
-    for i in (0, 3, 1, 2):
+    for i in (3, 0, 2, 1):
         landed = rcv.at[i, pl.ds(0, 16 * (nm - 1)), :]
         pltpu.make_async_copy(landed, landed, a2a_recv.at[i]).wait()
         v = silu(dot(mix_ref[...], rcv[i]))
@@ -212,14 +209,10 @@
             hop.start()
             hops.append(hop)
         keep_latent(i, v)
-    for hop in hops:
-        hop.wait()
-    keep_latent(4, lath[0].astype(F32) * has_below)
-    keep_latent(-1, lath[1].astype(F32) * has_above)
-
     place = me * BLOCK - EDGE + lane128
     inside = jnp.where((place >= 0) & (place < cols), 1.0, 0.0)
-    for step in range(6):
+
+    def grow_one(step):
         v = silu(dot(d1_ref[...], latx[96 * step : 96 * step + 288, :])) * inside
         if step == 0:
             v = v * has_above
@@ -235,13 +228,30 @@
             upx[base + 32 : base + 64, :] = even.astype(BF16)
             upx[base + 64 : base + 96, :] = odd.astype(BF16)
             upx[base + 96 : base + 128, :] = turn(even, -1).astype(BF16)
-    for step in range(8):
+
+    def grow_two(step):
         v = dot(d2_ref[...], upx[128 * step : 128 * step + 384, :]).astype(BF16)
         for a in range(2):
             for q in range(4):
                 zz[16 * (2 * step + a) : 16 * (2 * step + a + 1), 128 * q : 128 * (q + 1)] = v[
                     16 * (4 * a + q) : 16 * (4 * a + q + 1)
                 ]
+
+    for step in (2, 3):
+        grow_one(step)
+    for step in (3, 4):
+        grow_two(step)
+    for hop in hops:
+        hop.wait()
+    keep_latent(4, lath[0].astype(F32) * has_below)
+    keep_latent(-1, lath[1].astype(F32) * has_above)
+    for step in (0, 1, 4, 5):
+        grow_one(step)
+    for step in (0, 1, 2, 5, 6, 7):
+        grow_two(step)
+    for i in range(4):
+        sent = snd.at[i, pl.ds(0, nm - 1)]
+        pltpu.make_async_copy(sent, sent, a2a_send.at[i]).wait()
     woven = dot(zz[...], one_hot((512, 256), lambda a, b: b == 4 * (a % 128 - EDGE) + a // 128))
     order = one_hot((256, 256), lambda a, b: b == (a % 16) * 16 + a // 16)
     out_ref[...] = dot(order, woven.astype(BF16)).astype(BF16).reshape(16, 16, 256)

time: 41.5 us -> 35.9 us (0.87)
  Pallas kernels: 39.9 us -> 34.3 us
    pallas_call x1, Pallas kernels: 39.9 us -> 34.3 us  [per_device(): pl.pallas_call(body, out_shape=jax.ShapeDtypeStruct((16, 16, 4 * BLOCK),...]
where the time goes in v3:
time: 35.9 us; the launch traced here: 35.8 us
  Pallas kernels  34.3 us (96%)
  local copies, waits for them, and re-layouts  1.57 us (4%)
    pallas_call x1, Pallas kernels, per_device(): pl.pallas_call(body, out_shape=jax.ShapeDtypeStruct((16, 16, 4 * BLOCK),...  34.3 us
    unnamed x1, local copies, waits for them, and re-layouts  1.57 us

profile of v3, /device:TPU:1, one launch (start us, length us, event | category | flops | bytes accessed | tf_op | source)
XLA Modules:
  0.0 35.8 jit_solution(3564828036994538789)
XLA Ops:
  0.0 34.3 %shard_map.73 = bf16[16,16,256]{2,1,0:T(8,128)(2,1)} custom-call(bf16[5,16,4096]{2,1,0:T(8,128)(2,1)} %bitcast.6, bf16[5,3,3,64]{3,2,1,0:T(4,128)(2,1)} %bitcast.11, bf16[3,3,64,64]{3,2,1,0:T(8,128)(2,1)} %bitcast.7, bf16[3,3,16,64]{3,2,1,0:T(8,128)(2,1)} %bitcast.10, bf16[32,256]{1,0:T(8,128)(2,1)} %refs_4_.1, bf16[32,4,4,32]{3,2,1,0:T(4,128)(2,1)} %bitcast.8, ...), custom_call_target="tpu_custom_call" | custom-call | tf_op jit(solution)/shard_map/pallas_call | solution.py:324
  34.3 1.6 %copy.9 = bf16[16,16,256]{2,1,0:T(8,128)(2,1)} copy(bf16[16,16,256]{2,1,0:T(8,128)(2,1)} %shard_map.73) | data formatting | bytes 262144

commit v4 on v3

--- a/solution.py
+++ b/solution.py
@@ -154,9 +154,8 @@
 
     for t in range(3, 10):
         encode_one(t)
-    for t in range(3, 8):
-        encode_two(t)
-    encode_three(2)
+    encode_two(6)
+    encode_two(7)
 
     down.wait()
     up.wait()
@@ -180,7 +179,10 @@
     encode_two(1)
     encode_two(2)
     encode_three(0)
+    for t in (3, 4, 5):
+        encode_two(t)
     encode_three(1)
+    encode_three(2)
 
     def turn(v, by):
         return pltpu.roll(v, by % 128, 1)
@@ -195,7 +197,7 @@
     latx[672:768, :] = jnp.zeros((96, 128), BF16)
 
     hops = []
-    for i in (3, 0, 2, 1):
+    for i in (3, 0, 1, 2):
         landed = rcv.at[i, pl.ds(0, 16 * (nm - 1)), :]
         pltpu.make_async_copy(landed, landed, a2a_recv.at[i]).wait()
         v = silu(dot(mix_ref[...], rcv[i]))

time: 35.9 us -> 37.1 us (1.033)
  Pallas kernels: 34.3 us -> 35.4 us
    pallas_call x1, Pallas kernels: 34.3 us -> 35.4 us  [per_device(): pl.pallas_call(body, out_shape=jax.ShapeDtypeStruct((16, 16, 4 * BLOCK),...]
where the time goes in v4:
time: 37.1 us; the launch traced here: 37 us
  Pallas kernels  35.4 us (95%)
  local copies, waits for them, and re-layouts  1.57 us (4%)
    pallas_call x1, Pallas kernels, per_device(): pl.pallas_call(body, out_shape=jax.ShapeDtypeStruct((16, 16, 4 * BLOCK),...  35.4 us
    unnamed x1, local copies, waits for them, and re-layouts  1.57 us

profile of v4, /device:TPU:1, one launch (start us, length us, event | category | flops | bytes accessed | tf_op | source)
XLA Modules:
  0.0 37.0 jit_solution(14569153075682320002)
XLA Ops:
  0.0 35.4 %shard_map.73 = bf16[16,16,256]{2,1,0:T(8,128)(2,1)} custom-call(bf16[5,16,4096]{2,1,0:T(8,128)(2,1)} %bitcast.6, bf16[5,3,3,64]{3,2,1,0:T(4,128)(2,1)} %bitcast.11, bf16[3,3,64,64]{3,2,1,0:T(8,128)(2,1)} %bitcast.7, bf16[3,3,16,64]{3,2,1,0:T(8,128)(2,1)} %bitcast.10, bf16[32,256]{1,0:T(8,128)(2,1)} %refs_4_.1, bf16[32,4,4,32]{3,2,1,0:T(4,128)(2,1)} %bitcast.8, ...), custom_call_target="tpu_custom_call" | custom-call | tf_op jit(solution)/shard_map/pallas_call | solution.py:326
  35.4 1.6 %copy.9 = bf16[16,16,256]{2,1,0:T(8,128)(2,1)} copy(bf16[16,16,256]{2,1,0:T(8,128)(2,1)} %shard_map.73) | data formatting | bytes 262144

commit v5 on v3

--- a/solution.py
+++ b/solution.py
@@ -47,22 +47,23 @@
             barrier, inc=1, device_id={"mem": lax.rem(me + step, nm)}, device_id_type=MESH
         )
 
+    pl.semaphore_wait(barrier, nm + 1)
+
+    down = pltpu.make_async_remote_copy(
+        x_ref.at[:, pl.ds(8, 8), :], top, halo_send.at[0], halo_recv.at[0],
+        device_id={"row": below}, device_id_type=MESH,
+    )
+    up = pltpu.make_async_remote_copy(
+        x_ref.at[:, pl.ds(0, 8), :], bot, halo_send.at[1], halo_recv.at[1],
+        device_id={"row": above}, device_id_type=MESH,
+    )
+    down.start()
+    up.start()
+
     weights(
         first_ref, second_ref, third_ref, grow_one_ref, grow_two_ref,
         w1_ref, w2_ref, w3_ref, d1_ref, d2_ref,
     )
-    pl.semaphore_wait(barrier, nm + 1)
-
-    down = pltpu.make_async_remote_copy(
-        x_ref.at[:, pl.ds(8, 8), :], top, halo_send.at[0], halo_recv.at[0],
-        device_id={"row": below}, device_id_type=MESH,
-    )
-    up = pltpu.make_async_remote_copy(
-        x_ref.at[:, pl.ds(0, 8), :], bot, halo_send.at[1], halo_recv.at[1],
-        device_id={"row": above}, device_id_type=MESH,
-    )
-    down.start()
-    up.start()
 
     has_above = jnp.where(row > 0, 1.0, 0.0)
     has_below = jnp.where(row < nr - 1, 1.0, 0.0)

time: 35.9 us -> 36 us (level)
  no operation moved by 1% of the time
where the time goes in v5:
time: 36 us; the launch traced here: 35.8 us
  Pallas kernels  34.3 us (95%)
  local copies, waits for them, and re-layouts  1.57 us (4%)
    pallas_call x1, Pallas kernels, per_device(): pl.pallas_call(body, out_shape=jax.ShapeDtypeStruct((16, 16, 4 * BLOCK),...  34.3 us
    unnamed x1, local copies, waits for them, and re-layouts  1.57 us

profile of v5, /device:TPU:1, one launch (start us, length us, event | category | flops | bytes accessed | tf_op | source)
XLA Modules:
  0.0 35.8 jit_solution(3757250815683589546)
XLA Ops:
  0.0 34.3 %shard_map.73 = bf16[16,16,256]{2,1,0:T(8,128)(2,1)} custom-call(bf16[5,16,4096]{2,1,0:T(8,128)(2,1)} %bitcast.6, bf16[5,3,3,64]{3,2,1,0:T(4,128)(2,1)} %bitcast.11, bf16[3,3,64,64]{3,2,1,0:T(8,128)(2,1)} %bitcast.7, bf16[3,3,16,64]{3,2,1,0:T(8,128)(2,1)} %bitcast.10, bf16[32,256]{1,0:T(8,128)(2,1)} %refs_4_.1, bf16[32,4,4,32]{3,2,1,0:T(4,128)(2,1)} %bitcast.8, ...), custom_call_target="tpu_custom_call" | custom-call | tf_op jit(solution)/shard_map/pallas_call | solution.py:325
  34.3 1.6 %copy.9 = bf16[16,16,256]{2,1,0:T(8,128)(2,1)} copy(bf16[16,16,256]{2,1,0:T(8,128)(2,1)} %shard_map.73) | data formatting | bytes 262144
